TPU v7x, 32 devices: a whole 2x2x4 slice. The times are simulated.
32 devices in a mesh: ctx: 4 (over z), section: 2 (over x), mp: 4 (over y, core).
Axes of the slice: x: 2, y: 2, z: 4, core: 2. Of those that a mesh axis runs over, the one named last changes fastest.
Arguments:
- patches: bfloat16 [2, 768, 3200], P(None, ('ctx', 'mp')), may hold values from -16 to 16
- carried: bfloat16 [768, 3200], P(('ctx', 'mp')), may hold values from -16 to 16
- norm_gain: float32 [2, 3200], P('section'), may hold values from 0.1 to 1.9
- q_gain: float32 [2, 128], P('section'), may hold values from 1.5 to 2.5
- k_gain: float32 [2, 128], P('section'), may hold values from 1.5 to 2.5
- q_weight: bfloat16 [2, 3200, 2048], P('section', None, 'mp'), may hold values from -0.109375 to 0.109375
- k_weight: bfloat16 [2, 3200, 2048], P('section', None, 'mp'), may hold values from -0.109375 to 0.109375
- v_weight: bfloat16 [2, 3200, 2048], P('section', None, 'mp'), may hold values from -0.109375 to 0.109375
- o_weight: bfloat16 [2, 2048, 3200], P('section', 'mp', 'ctx'), may hold values from -0.125 to 0.125
Outputs:
- section_outputs: bfloat16 [2, 2, 768, 3200], P('section', None, ('ctx', 'mp'))
All inputs are finite; a program needn't handle non-finite values.
Results may differ from a plain program's by a relative error of at most 0.0063.
Values may be sent and summed in bfloat16 or wider, within the bound.
A program may use at most 128 MiB of HBM per device.

v0:
```python
import math

import jax
import jax.numpy as jnp
from jax import lax
from jax.sharding import PartitionSpec as P

epsilon = 1e-06


def shifted(value, axis, steps):
    count = lax.axis_size(axis)
    leading, last = (max(0, -steps), min(count, count - steps))
    return lax.ppermute(value, axis, [(source, source + steps) for source in range(leading, last)])


def rms_scaled(values, gain):
    return values * lax.rsqrt(jnp.mean(values * values, axis=-1, keepdims=True) + epsilon) * gain


def per_device(patches, carried, norm_gain, q_gain, k_gain, q_weight, k_weight, v_weight, o_weight):
    micro_count = patches.shape[0]
    head_dim = q_gain.shape[1]
    head_count = q_weight.shape[2] // head_dim
    columns = head_count * head_dim
    score_scale = 1.0 / math.sqrt(head_dim)
    section_index = lax.axis_index("section")
    layer_gain = norm_gain[0]
    query_gain = q_gain[0]
    key_gain = k_gain[0]
    incoming = carried
    results = []
    for micro_step in range(micro_count):
        layer_input = jnp.where(section_index == 0, patches[micro_step], incoming)
        residual = layer_input.astype(jnp.float32)
        normed = rms_scaled(residual, layer_gain).astype(jnp.bfloat16)
        project_segment = lax.all_gather(normed, "mp", axis=0, tiled=True)
        project_count = project_segment.shape[0]
        raw_query = jnp.dot(project_segment, q_weight[0], preferred_element_type=jnp.float32)
        raw_key = jnp.dot(project_segment, k_weight[0], preferred_element_type=jnp.float32)
        raw_value = jnp.dot(project_segment, v_weight[0], preferred_element_type=jnp.float32)
        query_rows = rms_scaled(
            raw_query.reshape(project_count, head_count, head_dim), query_gain
        ).reshape(project_count, columns)
        key_rows = rms_scaled(
            raw_key.reshape(project_count, head_count, head_dim), key_gain
        ).reshape(project_count, columns)
        projected = jnp.stack(
            (
                query_rows.astype(jnp.bfloat16),
                key_rows.astype(jnp.bfloat16),
                raw_value.astype(jnp.bfloat16),
            ),
            0,
        )
        block_count = projected.shape[1]
        attend_queries = projected[0].reshape(block_count, head_count, head_dim)
        key_block = lax.all_gather(projected[1], "ctx", axis=0, tiled=True)
        count = key_block.shape[0]
        scores = (
            jnp.einsum(
                "qhd,khd->qhk",
                attend_queries,
                key_block.reshape(count, head_count, head_dim),
                preferred_element_type=jnp.float32,
            )
            * score_scale
        )
        probs = jnp.exp(scores)
        totals = jnp.sum(probs, axis=2)
        weighted = jnp.einsum(
            "qhk,khd->qhd",
            probs.astype(jnp.bfloat16),
            lax.all_gather(projected[2], "ctx", axis=0, tiled=True).reshape(
                count, head_count, head_dim
            ),
            preferred_element_type=jnp.float32,
        )
        attended = (
            (weighted / totals[:, :, None]).reshape(block_count, columns).astype(jnp.bfloat16)
        )
        partial_value = jnp.dot(
            attended,
            lax.all_gather(o_weight[0], "ctx", axis=1, tiled=True),
            preferred_element_type=jnp.float32,
        )
        summed = lax.psum_scatter(partial_value, "mp", scatter_dimension=0, tiled=True)
        layer_out = (residual + summed).astype(jnp.bfloat16)
        results.append(layer_out)
        if micro_step + 1 < micro_count:
            incoming = shifted(layer_out, "section", 1)
    return jnp.stack(results)[None]


def solution(mesh):
    in_specs = (
        P(None, ("ctx", "mp"), None),
        P(("ctx", "mp"), None),
        P("section", None),
        P("section", None),
        P("section", None),
        P("section", None, "mp"),
        P("section", None, "mp"),
        P("section", None, "mp"),
        P("section", "mp", "ctx"),
    )
    out_specs = P("section", None, ("ctx", "mp"), None)
    return jax.shard_map(
        per_device, mesh=mesh, in_specs=in_specs, out_specs=out_specs, check_vma=False
    )
```

profile of v0, /device:TPU:0, one launch (start us, length us, event | category | flops | bytes accessed | tf_op | source)
XLA Modules:
  0.0 286.1 jit_solution(7352324095041157773)
XLA Ops:
  6.5 2.0 fusion.34
  8.6 0.8 reduce
  9.4 1.8 fusion.36
  11.2 0.0 all-gather.5.cloned.1.call-update
  11.2 0.0 all-gather.9.cloned.1.call-start
  11.3 0.7 all-gather.9.cloned.1.call-update
  12.0 0.0 reduce-scatter.3.cloned.1.call-start
  12.0 5.6 %copy.32 = bf16[512,3200]{1,0:T(8,128)(2,1)} copy(bf16[512,3200]{0,1:T(8,128)(2,1)} %bitcast.129) | data formatting | bytes 6553600 | tf_op jit(solution)/shard_map/dot_general | solution.py:40
  17.6 5.8 %copy.33 = bf16[512,3200]{1,0:T(8,128)(2,1)} copy(bf16[512,3200]{0,1:T(8,128)(2,1)} %bitcast.130) | data formatting | bytes 6553600 | tf_op jit(solution)/shard_map/dot_general | solution.py:39
  23.5 8.4 %all-gather.5.cloned.1.call-done = bf16[192,3200]{1,0:T(8,128)(2,1)} async-done(((bf16[48,3200]{1,0:T(8,128)(2,1)}), bf16[192,3200]{1,0:T(8,128)(2,1)}) %all-gather.5.cloned.1.call-update) | async-done | bytes 1228816 | tf_op jit(solution)/shard_map/all_gather | solution.py:37
  31.9 3.7 %multiply_reduce_fusion.3 = (f32[192,4]{0,1:T(4,128)S(1)}, f32[192,4,128]{2,0,1:T(8,128)S(1)}) fusion(bf16[4,128,3200]{2,1,0:T(8,128)(2,1)} %bitcast.131, bf16[192,3200]{1,0:T(8,128)(2,1)} %all-gather.5.cloned.1.call-done), kind=kOutput, calls=%fused_computation.60 | convolution fusion | flops 629341440 | bytes 4901888 | tf_op jit(solution)/shard_map/dot_general | solution.py:40
  35.6 0.2 copy_bitcast_fusion.1
  35.8 28.3 %all_gather.24 = bf16[768,512]{1,0:T(8,128)(2,1)} all-gather(bf16[192,512]{1,0:T(8,128)(2,1)S(1)} %copy_bitcast_fusion.1), channel_id=1, replica_groups=mesh['ctx'=4,'section'=2,'mp'=4] {'ctx'}, dimensions={0}, use_global_device_ids=true | all-gather | bytes 983040 | tf_op jit(solution)/shard_map/all_gather | solution.py:58
  64.1 2.3 copy.18
  66.4 3.8 %multiply_reduce_fusion.2 = (f32[192,4]{0,1:T(4,128)S(1)}, f32[192,4,128]{2,0,1:T(8,128)S(1)}) fusion(bf16[4,128,3200]{2,1,0:T(8,128)(2,1)} %bitcast.133, bf16[192,3200]{1,0:T(8,128)(2,1)} %all-gather.5.cloned.1.call-done), kind=kOutput, calls=%fused_computation.58 | convolution fusion | flops 629341440 | bytes 4901888 | tf_op jit(solution)/shard_map/dot_general | solution.py:39
  70.3 0.8 fusion.22
  71.1 30.4 %all_gather.23 = bf16[768,512]{1,0:T(8,128)(2,1)S(1)} all-gather(bf16[192,512]{1,0:T(8,128)(2,1)S(1)} %fusion.22), channel_id=1, replica_groups=mesh['ctx'=4,'section'=2,'mp'=4] {'ctx'}, dimensions={0}, use_global_device_ids=true | all-gather | bytes 983040 | tf_op jit(solution)/shard_map/all_gather | solution.py:74
  101.5 0.7 bitcast_reduce_fusion.1
  102.2 0.5 fusion.28
  102.7 16.9 %all-gather.9.cloned.1.call-done = bf16[1,512,3200]{1,2,0:T(8,128)(2,1)} async-done(((bf16[1,512,800]{1,2,0:T(8,128)(2,1)}), bf16[1,512,3200]{1,2,0:T(8,128)(2,1)}) %all-gather.9.cloned.1.call-update) | async-done | bytes 3276816 | tf_op jit(solution)/shard_map/all_gather | solution.py:84
  119.7 4.6 %fusion.2 = f32[192,3200]{1,0:T(8,128)} fusion(bf16[1,512,3200]{1,2,0:T(8,128)(2,1)} %all-gather.9.cloned.1.call-done, bf16[4,24,8,128]{3,2,1,0:T(8,128)(2,1)S(1)} %fusion.28), kind=kOutput, calls=%fused_computation.2 | convolution fusion | flops 629145600 | bytes 5931008 | tf_op jit(solution)/shard_map/dot_general | solution.py:82
  124.3 0.0 reduce-scatter.3.cloned.1.call-update
  124.3 0.0 all-gather.7.cloned.1.call-start
  124.3 32.9 %reduce-scatter.3.cloned.1.call-done = f32[48,3200]{1,0:T(8,128)} async-done(((f32[192,3200]{1,0:T(8,128)}), f32[48,3200]{1,0:T(8,128)}) %reduce-scatter.3.cloned.1.call-update) | async-done | bytes 614416 | tf_op jit(solution)/shard_map/reduce_scatter | solution.py:87
  157.2 1.2 fusion.37
  158.4 3.4 %collective-permute-start = (bf16[48,3200]{1,0:T(8,128)(2,1)S(1)}, bf16[48,3200]{1,0:T(8,128)(2,1)S(1)}, u32[]{:S(2)}, u32[]{:S(2)}) collective-permute-start(bf16[48,3200]{1,0:T(8,128)(2,1)S(1)} %fusion.37), channel_id=1, source_target_pairs={{0,4},{1,5},{2,6},{3,7},{8,12},{9,13},{10,14},{11,15},{16,20},{17,... | collective-permute-start | bytes 921608 | tf_op jit(solution)/shard_map/ppermute | solution.py:14
  161.8 6.5 %collective-permute-done = bf16[48,3200]{1,0:T(8,128)(2,1)S(1)} collective-permute-done((bf16[48,3200]{1,0:T(8,128)(2,1)S(1)}, bf16[48,3200]{1,0:T(8,128)(2,1)S(1)}, u32[]{:S(2)}, u32[]{:S(2)}) %collective-permute-start) | collective-permute-done | bytes 307232 | tf_op jit(solution)/shard_map/ppermute | solution.py:14
  168.3 1.2 fusion.38
  169.5 0.7 copy-done.5
  170.2 0.9 fusion.40
  171.1 0.0 all-gather.7.cloned.1.call-update
  171.1 0.0 reduce-scatter.5.cloned.1.call-start
  171.1 18.8 %all-gather.7.cloned.1.call-done = bf16[192,3200]{1,0:T(8,128)(2,1)} async-done(((bf16[48,3200]{1,0:T(8,128)(2,1)}), bf16[192,3200]{1,0:T(8,128)(2,1)}) %all-gather.7.cloned.1.call-update) | async-done | bytes 1228816 | tf_op jit(solution)/shard_map/all_gather | solution.py:37
  190.0 4.4 %multiply_reduce_fusion = (f32[192,4]{0,1:T(4,128)S(1)}, f32[192,4,128]{2,0,1:T(8,128)}) fusion(bf16[4,128,3200]{2,1,0:T(8,128)(2,1)} %bitcast.134, bf16[192,3200]{1,0:T(8,128)(2,1)} %all-gather.7.cloned.1.call-done), kind=kOutput, calls=%fused_computation.54 | convolution fusion | flops 629341440 | bytes 4901888 | tf_op jit(solution)/shard_map/dot_general | solution.py:39
  194.4 1.4 multiply_reduce_fusion.1
  195.8 0.2 copy_bitcast_fusion
  196.0 19.9 %all_gather.28 = bf16[768,512]{1,0:T(8,128)(2,1)} all-gather(bf16[192,512]{1,0:T(8,128)(2,1)S(1)} %copy_bitcast_fusion), channel_id=1, replica_groups=mesh['ctx'=4,'section'=2,'mp'=4] {'ctx'}, dimensions={0}, use_global_device_ids=true | all-gather | bytes 983040 | tf_op jit(solution)/shard_map/all_gather | solution.py:58
  216.0 2.3 copy.25
  218.3 2.2 fusion.25
  220.5 18.2 %all_gather.27 = bf16[768,512]{1,0:T(8,128)(2,1)S(1)} all-gather(bf16[192,512]{1,0:T(8,128)(2,1)S(1)} %fusion.25), channel_id=1, replica_groups=mesh['ctx'=4,'section'=2,'mp'=4] {'ctx'}, dimensions={0}, use_global_device_ids=true | all-gather | bytes 983040 | tf_op jit(solution)/shard_map/all_gather | solution.py:74
  238.7 0.7 bitcast_reduce_fusion
  239.4 0.5 fusion.29
  239.9 1.4 copy-done.1
  241.3 2.7 fusion
  244.0 0.0 reduce-scatter.5.cloned.1.call-update
  244.0 32.5 %reduce-scatter.5.cloned.1.call-done = f32[48,3200]{1,0:T(8,128)} async-done(((f32[192,3200]{1,0:T(8,128)}), f32[48,3200]{1,0:T(8,128)}) %reduce-scatter.5.cloned.1.call-update) | async-done | bytes 614416 | tf_op jit(solution)/shard_map/reduce_scatter | solution.py:87
  276.5 1.2 fusion.42
  277.7 1.9 maximum_bitcast_fusion
  (29 shorter events, 0.1 us)
Async XLA Ops:
  6.5 63.7 %copy-start = (bf16[1,3200,512]{2,1,0:T(8,128)(2,1)S(1)}, bf16[1,3200,512]{2,1,0:T(8,128)(2,1)}, u32[]{:S(2)}) copy-start(bf16[1,3200,512]{2,1,0:T(8,128)(2,1)} %param.16) | copy-start | bytes 9830404
  6.5 25.4 %all-gather.5.cloned.1.call-start = ((), (), s32[]{:S(2)}) async-start(), calls=%async_computation.2 | async-start | bytes 1536000 | tf_op jit(solution)/shard_map/all_gather | solution.py:37
  11.2 108.5 %all-gather.9.cloned.1.call-start = ((), (), s32[]{:S(2)}) async-start(), calls=%async_computation.6 | async-start | bytes 4096000 | tf_op jit(solution)/shard_map/all_gather | solution.py:84
  12.0 145.2 %reduce-scatter.3.cloned.1.call-start = ((), (), s32[]{:S(2)}) async-start(), calls=%async_computation.3 | async-start | bytes 3072000 | tf_op jit(solution)/shard_map/reduce_scatter | solution.py:87
  31.9 3.7 %copy-start.8 = (f32[1,128]{1,0:T(1,128)S(1)}, f32[1,128]{1,0:T(1,128)}, u32[]{:S(2)}) copy-start(f32[1,128]{1,0:T(1,128)} %param.13) | copy-start | bytes 1540
  66.4 3.8 %copy-start.10 = (bf16[192,3200]{1,0:T(8,128)(2,1)S(1)}, bf16[192,3200]{1,0:T(8,128)(2,1)}, u32[]{:S(2)}) copy-start(bf16[192,3200]{1,0:T(8,128)(2,1)} %all-gather.5.cloned.1.call-done) | copy-start | bytes 3686404
  70.3 31.3 %copy-start.3 = (bf16[768,512]{0,1:T(8,128)(2,1)S(1)}, bf16[768,512]{0,1:T(8,128)(2,1)}, u32[]{:S(2)}) copy-start(bf16[768,512]{0,1:T(8,128)(2,1)} %copy.18) | copy-start | bytes 2359300
  70.3 31.3 %copy-start.9 = (f32[1,128]{1,0:T(1,128)S(1)}, f32[1,128]{1,0:T(1,128)}, u32[]{:S(2)}) copy-start(f32[1,128]{1,0:T(1,128)} %param.12) | copy-start | bytes 1540
  124.3 65.7 %all-gather.7.cloned.1.call-start = ((), (), s32[]{:S(2)}) async-start(), calls=%async_computation.4 | async-start | bytes 1536000 | tf_op jit(solution)/shard_map/all_gather | solution.py:37
  158.4 3.4 %copy-start.6 = (bf16[48,3200]{1,0:T(8,128)(2,1)}, bf16[48,3200]{1,0:T(8,128)(2,1)S(1)}, u32[]{:S(2)}) copy-start(bf16[48,3200]{1,0:T(8,128)(2,1)S(1)} %fusion.37) | copy-start | bytes 921604
  158.4 9.9 %collective-permute-start = (bf16[48,3200]{1,0:T(8,128)(2,1)S(1)}, bf16[48,3200]{1,0:T(8,128)(2,1)S(1)}, u32[]{:S(2)}, u32[]{:S(2)}) collective-permute-start(bf16[48,3200]{1,0:T(8,128)(2,1)S(1)} %fusion.37), channel_id=1, source_target_pairs={{0,4},{1,5},{2,6},{3,7},{8,12},{9,13},{10,14},{11,15},{16,20},{17,... | collective-permute-start | bytes 921608 | tf_op jit(solution)/shard_map/ppermute | solution.py:14
  169.5 0.7 copy-start.5
  171.1 105.4 %reduce-scatter.5.cloned.1.call-start = ((), (), s32[]{:S(2)}) async-start(), calls=%async_computation.5 | async-start | bytes 3072000 | tf_op jit(solution)/shard_map/reduce_scatter | solution.py:87
  190.0 4.4 %copy-start.2 = (bf16[512,3200]{1,0:T(8,128)(2,1)S(1)}, bf16[512,3200]{1,0:T(8,128)(2,1)}, u32[]{:S(2)}) copy-start(bf16[512,3200]{1,0:T(8,128)(2,1)} %copy.32) | copy-start | bytes 9830404
  190.0 4.4 %copy-start.11 = (bf16[192,3200]{1,0:T(8,128)(2,1)S(1)}, bf16[192,3200]{1,0:T(8,128)(2,1)}, u32[]{:S(2)}) copy-start(bf16[192,3200]{1,0:T(8,128)(2,1)} %all-gather.7.cloned.1.call-done) | copy-start | bytes 3686404
  218.3 20.4 %copy-start.4 = (bf16[768,512]{0,1:T(8,128)(2,1)S(1)}, bf16[768,512]{0,1:T(8,128)(2,1)}, u32[]{:S(2)}) copy-start(bf16[768,512]{0,1:T(8,128)(2,1)} %copy.25) | copy-start | bytes 2359300
  218.3 20.4 %copy-start.7 = (f32[192,4,128]{2,0,1:T(8,128)S(1)}, f32[192,4,128]{2,0,1:T(8,128)}, u32[]{:S(2)}) copy-start(f32[192,4,128]{2,0,1:T(8,128)} %get-tuple-element.18) | copy-start | bytes 1179652
  239.4 1.9 copy-start.1
Sparse Core Ops, SparseCore 0:
  11.3 20.5 all-gather.4
  33.5 86.1 all-gather.8
  124.4 32.7 reduce-scatter.2
  171.2 18.7 all-gather.6
  244.1 32.2 reduce-scatter.4
where the time goes:
time: 287 us; the launch traced here: 286 us
  waiting for transfers between devices  117 us (41%)
  blocking collectives  96.9 us (34%)
  matrix products  26 us (9%)
  local copies, waits for them, and re-layouts  18.2 us (6%)
  between operations  13.3 us (5%)
  other arithmetic  11.3 us (4%)
  starting transfers between devices  3.54 us (1%)
    reduce_scatter x2, waiting for transfers between devices, per_device(): lax.psum_scatter(partial_value, 'mp', scatter_dimension=0, tiled=True)  65.3 us
    all_gather x2, blocking collectives, per_device(): lax.all_gather(projected[2], 'ctx', axis=0, tiled=True)  48.6 us
    all_gather x2, blocking collectives, per_device(): key_block = lax.all_gather(projected[1], 'ctx', axis=0, tiled=True)  48.3 us
    all_gather x2, waiting for transfers between devices, per_device(): project_segment = lax.all_gather(normed, 'mp', axis=0, tiled=True)  27.3 us
    all_gather x1, waiting for transfers between devices, per_device(): lax.all_gather(o_weight[0], 'ctx', axis=1, tiled=True)  16.9 us
    dot_general x2, matrix products, per_device(): jnp.dot(project_segment, q_weight[0], preferred_element_type=jnp.float32)  8.21 us
    dot_general x2, matrix products, per_device(): jnp.dot(attended, lax.all_gather(o_weight[0], 'ctx', axis=1, tiled=True),...  7.24 us
    ppermute x1, waiting for transfers between devices, shifted(): lax.ppermute(value, axis, [(source, source + steps) for source in range(l...  6.49 us
  transfers between devices with their start and end apart: 6, of which 6 were waited for; matrix products, arithmetic and copies ran while one was open for 8% of the time, Pallas kernels for 0%

commit v1 on v0

v1 whole, which is shorter than its diff:
```python
import functools
import math

import jax
import jax.numpy as jnp
from jax import lax
from jax.experimental import pallas as pl
from jax.experimental.pallas import tpu as pltpu
from jax.sharding import PartitionSpec as P

epsilon = 1e-06


def rms_scaled(values, gain):
    return values * lax.rsqrt(jnp.mean(values * values, axis=-1, keepdims=True) + epsilon) * gain


def shifted(value, axis, steps):
    count = lax.axis_size(axis)
    leading, last = (max(0, -steps), min(count, count - steps))
    return lax.ppermute(value, axis, [(source, source + steps) for source in range(leading, last)])


def per_device(patches, carried, norm_gain, q_gain, k_gain, q_weight, k_weight, v_weight, o_weight):
    micro_count = patches.shape[0]
    head_dim = q_gain.shape[1]
    head_count = q_weight.shape[2] // head_dim
    columns = head_count * head_dim
    score_scale = 1.0 / math.sqrt(head_dim)
    section_index = lax.axis_index("section")
    incoming = carried
    results = []
    out_weight = lax.all_gather(o_weight[0], "ctx", axis=1, tiled=True)
    for micro_step in range(micro_count):
        layer_input = jnp.where(section_index == 0, patches[micro_step], incoming)
        residual = layer_input.astype(jnp.float32)
        normed = rms_scaled(residual, norm_gain[0]).astype(jnp.bfloat16)
        segment = lax.all_gather(normed, "mp", axis=0, tiled=True)
        rows = segment.shape[0]
        raw_query = jnp.dot(segment, q_weight[0], preferred_element_type=jnp.float32)
        raw_key = jnp.dot(segment, k_weight[0], preferred_element_type=jnp.float32)
        raw_value = jnp.dot(segment, v_weight[0], preferred_element_type=jnp.float32)
        queries = rms_scaled(raw_query.reshape(rows, head_count, head_dim), q_gain[0])
        keys = rms_scaled(raw_key.reshape(rows, head_count, head_dim), k_gain[0])
        keys = keys.astype(jnp.bfloat16).reshape(rows, columns)
        key_block = lax.all_gather(keys, "ctx", axis=0, tiled=True)
        value_block = lax.all_gather(raw_value.astype(jnp.bfloat16), "ctx", axis=0, tiled=True)
        count = key_block.shape[0]
        scores = score_scale * jnp.einsum(
            "qhd,khd->qhk",
            queries.astype(jnp.bfloat16),
            key_block.reshape(count, head_count, head_dim),
            preferred_element_type=jnp.float32,
        )
        probs = jnp.exp(scores)
        totals = jnp.sum(probs, axis=2)
        weighted = jnp.einsum(
            "qhk,khd->qhd",
            probs.astype(jnp.bfloat16),
            value_block.reshape(count, head_count, head_dim),
            preferred_element_type=jnp.float32,
        )
        attended = (weighted / totals[:, :, None]).reshape(rows, columns).astype(jnp.bfloat16)
        partial_value = jnp.dot(attended, out_weight, preferred_element_type=jnp.float32)
        summed = lax.psum_scatter(partial_value, "mp", scatter_dimension=0, tiled=True)
        layer_out = (residual + summed).astype(jnp.bfloat16)
        results.append(layer_out)
        if micro_step + 1 < micro_count:
            incoming = shifted(layer_out, "section", 1)
    return jnp.stack(results)[None]


CHUNKS = 3


class Copies:
    def __init__(self, send_sems, recv_sems):
        self.send_sems, self.recv_sems, self.used = send_sems, recv_sems, 0

    def take(self, count):
        first = self.used
        self.used += count
        return first

    def make(self, index, source, target, device):
        return pltpu.make_async_remote_copy(
            src_ref=source,
            dst_ref=target,
            send_sem=self.send_sems.at[index],
            recv_sem=self.recv_sems.at[index],
            device_id=device,
            device_id_type=pl.DeviceIdType.MESH,
        )


def copies_needed(steps, ctx):
    return steps * (3 * CHUNKS + ctx + ctx * ctx + 3 * ctx) + (steps - 1) * CHUNKS


def layer_kernel(
    steps, ctx,
    patches, carried, norm_gain, q_gain, k_gain, q_weight, k_weight, v_weight, o_weight,
    out,
    xg, normed, wq, wk, wv, wo, heads, qkv, att, pair_out, pair_in, keep, far_out, far_in, fin_out, fin_in, outbuf,
    send_sems, recv_sems, load_sems,
):
    me_ctx = lax.axis_index("ctx")
    me_section = lax.axis_index("section")
    me_mp = lax.axis_index("mp")
    core_peer = {"mp": me_mp + 1 - 2 * lax.rem(me_mp, 2)}
    far_peer = {"mp": lax.rem(me_mp + 2, 4)}
    section_peer = {"section": 1 - me_section}

    def ctx_at(offset):
        return lax.rem(me_ctx + offset + ctx, ctx)

    head_dim = q_gain.shape[1]
    head_count = q_weight.shape[2] // head_dim
    rows = xg.shape[2]
    segment = 4 * rows
    scale = math.log2(math.e) / math.sqrt(head_dim)

    @pl.when(me_section == 0)
    def _():
        for t in range(steps):
            pltpu.make_async_copy(patches.at[t], xg.at[t, 0], load_sems.at[t]).start()

    @pl.when(me_section == 1)
    def _():
        pltpu.make_async_copy(carried, xg.at[0, 0], load_sems.at[0]).start()

    weight_loads = []
    for n, (source, target) in enumerate(((q_weight, wq), (k_weight, wk), (v_weight, wv))):
        weight_loads.append(pltpu.make_async_copy(source.at[0], target, load_sems.at[steps + n]))
    out_loads = []
    for e in range(ctx):
        first = pl.multiple_of(ctx_at(-e) * head_dim, head_dim)
        out_loads.append(
            pltpu.make_async_copy(
                o_weight.at[0, pl.ds(first, head_dim)],
                wo.at[pl.ds(e * head_dim, head_dim)],
                load_sems.at[steps + 3 + e],
            )
        )
    for load in weight_loads + out_loads:
        load.start()

    barrier = pltpu.get_barrier_semaphore()
    peers = [core_peer, far_peer, section_peer] + [{"ctx": ctx_at(d)} for d in range(1, ctx)]
    for peer in peers:
        pl.semaphore_signal(barrier, inc=1, device_id=peer, device_id_type=pl.DeviceIdType.MESH)
    pl.semaphore_wait(barrier, len(peers))

    copies = Copies(send_sems, recv_sems)
    sent = []
    handover = None
    chunk = rows // CHUNKS
    for t in range(steps):
        base = copies.take(3 * CHUNKS)
        near, far, relay = [], [], []
        for i in range(CHUNKS):
            part = pl.ds(i * chunk, chunk)
            far.append(copies.make(base + i, xg.at[t, 0, part], xg.at[t, 2, part], far_peer))
            near.append(copies.make(base + CHUNKS + i, xg.at[t, 0, part], xg.at[t, 1, part], core_peer))
            relay.append(copies.make(base + 2 * CHUNKS + i, xg.at[t, 2, part], xg.at[t, 3, part], core_peer))
        sent += far + near + relay

        if t == 0:
            pltpu.make_async_copy(carried, xg.at[0, 0], load_sems.at[0]).wait()
        else:
            @pl.when(me_section == 0)
            def _():
                pltpu.make_async_copy(patches.at[t], xg.at[t, 0], load_sems.at[t]).wait()

        for i in range(CHUNKS):
            if t > 0:
                incoming = handover[i]

                @pl.when(me_section == 1)
                def _():
                    incoming.wait_recv()

            far[i].start()
            near[i].start()

        def normalize(j):
            values = xg[t, j].astype(jnp.float32)
            normed[pl.ds(j * rows, rows)] = rms_scaled(values, norm_gain[...]).astype(jnp.bfloat16)

        normalize(0)
        for i in range(CHUNKS):
            far[i].wait_recv()
            relay[i].start()
        for i in range(CHUNKS):
            near[i].wait_recv()
        normalize(1)
        normalize(2)
        for i in range(CHUNKS):
            relay[i].wait_recv()
        normalize(3)

        if t == 0:
            for load in weight_loads:
                load.wait()
        base = copies.take(ctx)
        for first in range(0, head_count, 2):
            lanes = pl.ds(first * head_dim, 2 * head_dim)
            raw = [
                jnp.dot(normed[...], w[:, lanes], preferred_element_type=jnp.float32) for w in (wq, wk, wv)
            ]
            for h in (first, first + 1):
                own = slice((h - first) * head_dim, (h - first + 1) * head_dim)
                parts = (
                    rms_scaled(raw[0][:, own], q_gain[...]).astype(jnp.bfloat16),
                    rms_scaled(raw[1][:, own], k_gain[...]).astype(jnp.bfloat16),
                    raw[2][:, own].astype(jnp.bfloat16),
                )

                @pl.when(me_ctx == h)
                def _():
                    for n in range(3):
                        qkv[t, n, 0] = parts[n]

                @pl.when(me_ctx != h)
                def _():
                    for n in range(3):
                        heads[t, h, n] = parts[n]
                    d = lax.rem(h - me_ctx + ctx, ctx)
                    copies.make(base + d, heads.at[t, h], qkv.at[t, :, d], {"ctx": h}).start()

        arrivals = []
        for d in range(1, ctx):
            arrivals.append(copies.make(base + d, heads.at[t, ctx_at(d)], qkv.at[t, :, d], {"ctx": ctx_at(d)}))
        for arrival in arrivals:
            arrival.wait_recv()
        sent += arrivals

        base = copies.take(ctx * ctx)
        keys = qkv[t, 1].reshape(ctx * segment, head_dim)
        vals = qkv[t, 2].reshape(ctx * segment, head_dim)
        gathers = {}
        for d in range(ctx):
            k = (-d) % ctx
            scores = lax.dot_general(
                qkv[t, 0, d], keys, (((1,), (1,)), ((), ())), preferred_element_type=jnp.float32
            )
            probs = jnp.exp2(scores * scale)
            totals = jnp.sum(probs, axis=1, keepdims=True)
            weighted = jnp.dot(probs.astype(jnp.bfloat16), vals, preferred_element_type=jnp.float32)
            att[t, k, 0] = (weighted / totals).astype(jnp.bfloat16)
            for e in range(1, ctx):
                there = (k - e) % ctx
                copy = copies.make(
                    base + there * ctx + e, att.at[t, k, 0], att.at[t, there, e], {"ctx": ctx_at(e)}
                )
                copy.start()
                gathers[there, e] = copy
                sent.append(copy)

        if t == 0:
            for load in out_loads:
                load.wait()
        base = copies.take(3 * ctx)
        pairs, fars, lasts = {}, {}, {}

        def project(k):
            for e in range(1, ctx):
                gathers[k, e].wait_recv()
            lhs = jnp.concatenate([att[t, k, e] for e in range(ctx)], axis=1)
            product = jnp.dot(lhs, wo[...], preferred_element_type=jnp.float32)
            for n in range(2):
                keep[k, n] = product[2 * n * rows:(2 * n + 1) * rows]
                pair_out[t, k, n] = product[(2 * n + 1) * rows:(2 * n + 2) * rows].astype(jnp.bfloat16)
            pairs[k] = copies.make(base + k, pair_out.at[t, k], pair_in.at[t, k], core_peer)
            pairs[k].start()

        def sum_pair(k):
            pairs[k].wait_recv()
            far_out[t, k] = (keep[k, 1] + pair_in[t, k, 1].astype(jnp.float32)).astype(jnp.bfloat16)
            fars[k] = copies.make(base + ctx + k, far_out.at[t, k], far_in.at[t, k], far_peer)
            fars[k].start()
            keep[k, 0] = keep[k, 0] + pair_in[t, k, 0].astype(jnp.float32)

        def sum_far(k):
            fars[k].wait_recv()
            total = (keep[k, 0] + far_in[t, k].astype(jnp.float32)).astype(jnp.bfloat16)
            if k == 0:
                fin_in[t, me_ctx] = total
            else:
                fin_out[t, k] = total
                lasts[k] = copies.make(
                    base + 2 * ctx + k, fin_out.at[t, k], fin_in.at[t, me_ctx], {"ctx": ctx_at(k)}
                )
                lasts[k].start()

        order = list(range(1, ctx)) + [0]
        for n in range(ctx + 3):
            if n < ctx:
                project(order[n])
            if 1 <= n <= ctx:
                sum_pair(order[n - 1])
            if 3 <= n:
                sum_far(order[n - 3])
        sent += list(pairs.values()) + list(fars.values()) + list(lasts.values())
        for k in range(1, ctx):
            copies.make(
                base + 2 * ctx + k, fin_out.at[t, k], fin_in.at[t, ctx_at(-k)], {"ctx": ctx_at(k)}
            ).wait_recv()

        if t + 1 < steps:
            base = copies.take(CHUNKS)
            handover = []
        for i in range(CHUNKS):
            part = pl.ds(i * chunk, chunk)
            summed = jnp.concatenate([fin_in[t, c, part] for c in range(ctx)], axis=1)
            outbuf[t, part] = (xg[t, 0, part].astype(jnp.float32) + summed.astype(jnp.float32)).astype(jnp.bfloat16)
            if t + 1 < steps:
                copy = copies.make(base + i, outbuf.at[t, part], xg.at[t + 1, 0, part], section_peer)
                handover.append(copy)

                @pl.when(me_section == 0)
                def _():
                    copy.start()

        store = pltpu.make_async_copy(outbuf.at[t], out.at[0, t], load_sems.at[steps + 3 + ctx + t])
        store.start()
        if t + 1 == steps:
            for s in range(steps):
                pltpu.make_async_copy(outbuf.at[s], out.at[0, s], load_sems.at[steps + 3 + ctx + s]).wait()
        else:
            handed = handover

            @pl.when(me_section == 0)
            def _():
                for copy in handed:
                    copy.wait_send()

    for copy in sent:
        copy.wait_send()


def fused_device(patches, carried, norm_gain, q_gain, k_gain, q_weight, k_weight, v_weight, o_weight):
    steps, rows, width = patches.shape
    ctx = lax.axis_size("ctx")
    head_dim = q_gain.shape[1]
    columns = q_weight.shape[2]
    share = o_weight.shape[2]
    bf16, f32 = jnp.bfloat16, jnp.float32
    segment = 4 * rows
    anywhere = pl.BlockSpec(memory_space=pl.ANY)
    vmem = pl.BlockSpec(memory_space=pltpu.VMEM)
    number = copies_needed(steps, ctx)
    flops = steps * 2 * segment * (3 * width * columns + ctx * columns * share + 2 * ctx * segment * columns)
    return pl.pallas_call(
        functools.partial(layer_kernel, steps, ctx),
        out_shape=jax.ShapeDtypeStruct((1, steps, rows, width), bf16),
        in_specs=[anywhere, anywhere, vmem, vmem, vmem, anywhere, anywhere, anywhere, anywhere],
        out_specs=anywhere,
        scratch_shapes=[
            pltpu.VMEM((steps, 4, rows, width), bf16),
            pltpu.VMEM((segment, width), bf16),
            pltpu.VMEM((width, columns), bf16),
            pltpu.VMEM((width, columns), bf16),
            pltpu.VMEM((width, columns), bf16),
            pltpu.VMEM((columns, share), bf16),
            pltpu.VMEM((steps, ctx, 3, segment, head_dim), bf16),
            pltpu.VMEM((steps, 3, ctx, segment, head_dim), bf16),
            pltpu.VMEM((steps, ctx, ctx, segment, head_dim), bf16),
            pltpu.VMEM((steps, ctx, 2, rows, share), bf16),
            pltpu.VMEM((steps, ctx, 2, rows, share), bf16),
            pltpu.VMEM((ctx, 2, rows, share), f32),
            pltpu.VMEM((steps, ctx, rows, share), bf16),
            pltpu.VMEM((steps, ctx, rows, share), bf16),
            pltpu.VMEM((steps, ctx, rows, share), bf16),
            pltpu.VMEM((steps, ctx, rows, share), bf16),
            pltpu.VMEM((steps, rows, width), bf16),
            pltpu.SemaphoreType.DMA((number,)),
            pltpu.SemaphoreType.DMA((number,)),
            pltpu.SemaphoreType.DMA((2 * steps + 3 + ctx,)),
        ],
        compiler_params=pltpu.CompilerParams(
            collective_id=0, has_side_effects=True, vmem_limit_bytes=56 * 2**20
        ),
        cost_estimate=pl.CostEstimate(flops=flops, bytes_accessed=12 * 2**20, transcendentals=0),
    )(patches, carried, norm_gain, q_gain, k_gain, q_weight, k_weight, v_weight, o_weight)


def solution(mesh):
    in_specs = (
        P(None, ("ctx", "mp"), None),
        P(("ctx", "mp"), None),
        P("section", None),
        P("section", None),
        P("section", None),
        P("section", None, "mp"),
        P("section", None, "mp"),
        P("section", None, "mp"),
        P("section", "mp", "ctx"),
    )
    out_specs = P("section", None, ("ctx", "mp"), None)

    def program(*arrays):
        ctx, mp, sections = mesh.shape["ctx"], mesh.shape["mp"], mesh.shape["section"]
        heads = arrays[5].shape[2] // arrays[3].shape[1]
        rows = arrays[1].shape[0] // (ctx * mp)
        fits = mp == 4 and sections == 2 and ctx * mp == heads and ctx % 2 == 0 and rows == 16 * CHUNKS
        body = fused_device if fits else per_device
        return jax.shard_map(body, mesh=mesh, in_specs=in_specs, out_specs=out_specs, check_vma=False)(*arrays)

    return program
```

time: 287 us -> 130 us (0.45)
  Pallas kernels: 0 us -> 126 us
  waiting for transfers between devices: 117 us -> 0 us
  blocking collectives: 96.9 us -> 0 us
  matrix products: 26 us -> 0 us
  local copies, waits for them, and re-layouts: 18.2 us -> 4.15 us
  between operations: 13.3 us -> 0.01 us
  other arithmetic: 11.3 us -> 0 us
  starting transfers between devices: 3.54 us -> 0 us
    pallas_call x0 -> x1, Pallas kernels: none -> 126 us  [fused_device(): pl.pallas_call(functools.partial(layer_kernel, steps, ctx), out_shape=jax...]
    all_gather x4 -> x0, blocking collectives: 96.9 us -> none  [the longest x2 48.6 us: per_device(): lax.all_gather(projected[2], 'ctx', axis=0, tiled=True)]
    reduce_scatter x2 -> x0, waiting for transfers between devices: 65.3 us -> none  [per_device(): lax.psum_scatter(partial_value, 'mp', scatter_dimension=0, tiled=True)]
    all_gather x3 -> x0, waiting for transfers between devices: 44.2 us -> none  [the longest x2 27.3 us: per_device(): project_segment = lax.all_gather(normed, 'mp', axis=0, tiled=True)]
    dot_general x12 -> x0, matrix products: 26 us -> none  [the longest x2 8.21 us: per_device(): jnp.dot(project_segment, q_weight[0], preferred_element_type=jnp.float32)]
    dot_general x2 -> x0, local copies, waits for them, and re-layouts: 11.5 us -> none  [the longest x1 5.82 us: per_device(): jnp.dot(project_segment, q_weight[0], preferred_element_type=jnp.float32)]
    ppermute x1 -> x0, waiting for transfers between devices: 6.49 us -> none  [shifted(): lax.ppermute(value, axis, [(source, source + steps) for source in range(l...]
    all_gather x2 -> x0, local copies, waits for them, and re-layouts: 4.59 us -> none  [per_device(): key_block = lax.all_gather(projected[1], 'ctx', axis=0, tiled=True)]
  transfers between devices with their start and end apart: 6 -> 0, of which waited for: 6 -> 0; matrix products, arithmetic and copies ran while one was open for 8% -> 0% of each run, Pallas kernels for 0% -> 0%
where the time goes in v1:
time: 130 us
  Pallas kernels  126 us (97%)
  local copies, waits for them, and re-layouts  4.15 us (3%)
    pallas_call x1, Pallas kernels, fused_device(): pl.pallas_call(functools.partial(layer_kernel, steps, ctx), out_shape=jax...  126 us
    unnamed x2, local copies, waits for them, and re-layouts  4.15 us

profile of v1, /device:TPU:0, one launch (start us, length us, event | category | flops | bytes accessed | tf_op | source)
XLA Modules:
  0.0 129.7 jit_solution(3965650249778863970)
XLA Ops:
  0.0 2.2 %copy.10.o_weight = bf16[1,512,800]{2,1,0:T(8,128)(2,1)} copy(bf16[1,512,800]{1,2,0:T(8,128)(2,1)} %param.17) | data formatting | bytes 1638400 | tf_op args[8]
  2.2 125.5 %shard_map.91 = bf16[1,2,48,3200]{3,2,1,0:T(8,128)(2,1)} custom-call(bf16[2,48,3200]{2,1,0:T(8,128)(2,1)} %patches.1, bf16[48,3200]{1,0:T(8,128)(2,1)} %carried.1, f32[1,3200]{1,0:T(1,128)} %norm_gain.1, f32[1,128]{1,0:T(1,128)} %q_gain.1, f32[1,128]{1,0:T(1,128)} %k_gain.1, bf16[1,3200,512]{2,1,0:T(8,128)(2,1)} %q_weight.1, bf16[1,3200,512]{2,1,0:T(8,128)(2,1)} %k_weight.1, ...), custom_call_target="tpu_custom_call" | custom-call | flops 5637144576 | bytes 12582912 | tf_op jit(solution)/shard_map/pallas_call | solution.py:354
  127.8 1.9 %copy.12 = bf16[1,2,48,3200]{3,2,1,0:T(8,128)(2,1)} copy(bf16[1,2,48,3200]{3,2,1,0:T(8,128)(2,1)} %shard_map.91) | data formatting | bytes 1228800

commit v2 on v1

--- a/solution.py
+++ b/solution.py
@@ -94,14 +94,14 @@
 
 
 def copies_needed(steps, ctx):
-    return steps * (3 * CHUNKS + ctx + ctx * ctx + 3 * ctx) + (steps - 1) * CHUNKS
+    return steps * (3 * CHUNKS + 2 * ctx + ctx * ctx + 3 * ctx) + (steps - 1) * CHUNKS
 
 
 def layer_kernel(
     steps, ctx,
     patches, carried, norm_gain, q_gain, k_gain, q_weight, k_weight, v_weight, o_weight,
     out,
-    xg, normed, wq, wk, wv, wo, heads, qkv, att, pair_out, pair_in, keep, far_out, far_in, fin_out, fin_in, outbuf,
+    xg, normed, wq, wk, wv, wo_held, wo, heads, qkv, att, pair_out, pair_in, keep, far_out, far_in, fin_out, fin_in, outbuf,
     send_sems, recv_sems, load_sems,
 ):
     me_ctx = lax.axis_index("ctx")
@@ -114,6 +114,9 @@
     def ctx_at(offset):
         return lax.rem(me_ctx + offset + ctx, ctx)
 
+    def is_direct(offset):
+        return me_ctx != (ctx - 1 if offset == 1 else 0)
+
     head_dim = q_gain.shape[1]
     head_count = q_weight.shape[2] // head_dim
     rows = xg.shape[2]
@@ -137,8 +140,8 @@
         first = pl.multiple_of(ctx_at(-e) * head_dim, head_dim)
         out_loads.append(
             pltpu.make_async_copy(
-                o_weight.at[0, pl.ds(first, head_dim)],
-                wo.at[pl.ds(e * head_dim, head_dim)],
+                o_weight.at[0, :, pl.ds(first, head_dim)],
+                wo_held.at[e],
                 load_sems.at[steps + 3 + e],
             )
         )
@@ -152,7 +155,7 @@
     pl.semaphore_wait(barrier, len(peers))
 
     copies = Copies(send_sems, recv_sems)
-    sent = []
+    sent, skippable, relays = [], [], []
     handover = None
     chunk = rows // CHUNKS
     for t in range(steps):
@@ -191,6 +194,10 @@
         for i in range(CHUNKS):
             far[i].wait_recv()
             relay[i].start()
+        if t == 0:
+            for e in range(ctx):
+                out_loads[e].wait()
+                wo[pl.ds(e * head_dim, head_dim)] = wo_held[e].T
         for i in range(CHUNKS):
             near[i].wait_recv()
         normalize(1)
@@ -235,9 +242,10 @@
             arrival.wait_recv()
         sent += arrivals
 
-        base = copies.take(ctx * ctx)
+        base = gather_base = copies.take(ctx * ctx)
         keys = qkv[t, 1].reshape(ctx * segment, head_dim)
         vals = qkv[t, 2].reshape(ctx * segment, head_dim)
+        relay_base = copies.take(ctx)
         gathers = {}
         for d in range(ctx):
             k = (-d) % ctx
@@ -253,19 +261,42 @@
                 copy = copies.make(
                     base + there * ctx + e, att.at[t, k, 0], att.at[t, there, e], {"ctx": ctx_at(e)}
                 )
-                copy.start()
                 gathers[there, e] = copy
-                sent.append(copy)
-
-        if t == 0:
-            for load in out_loads:
-                load.wait()
+                if e in (1, ctx - 1):
+                    @pl.when(is_direct(e))
+                    def _():
+                        copy.start()
+
+                    skippable.append((e, copy))
+                else:
+                    copy.start()
+                    sent.append(copy)
+
         base = copies.take(3 * ctx)
         pairs, fars, lasts = {}, {}, {}
 
+        def relay_ends(k):
+            gathers[k, 2].wait_recv()
+            for r, to, e in ((1, 0, 1), (ctx - 2, ctx - 1, ctx - 1)):
+                there = (k + r - to) % ctx
+                copy = pltpu.make_async_remote_copy(
+                    src_ref=att.at[t, k, 2],
+                    dst_ref=att.at[t, there, e],
+                    send_sem=copies.send_sems.at[relay_base + k],
+                    recv_sem=copies.recv_sems.at[gather_base + there * ctx + e],
+                    device_id={"ctx": to},
+                    device_id_type=pl.DeviceIdType.MESH,
+                )
+                relays.append((r, copy))
+
+                @pl.when(me_ctx == r)
+                def _():
+                    copy.start()
+
         def project(k):
             for e in range(1, ctx):
-                gathers[k, e].wait_recv()
+                if e != 2:
+                    gathers[k, e].wait_recv()
             lhs = jnp.concatenate([att[t, k, e] for e in range(ctx)], axis=1)
             product = jnp.dot(lhs, wo[...], preferred_element_type=jnp.float32)
             for n in range(2):
@@ -294,9 +325,13 @@
                 lasts[k].start()
 
         order = list(range(1, ctx)) + [0]
+        relay_ends(2)
+        relay_ends(1)
         for n in range(ctx + 3):
             if n < ctx:
                 project(order[n])
+            if n < 2:
+                relay_ends((0, 3)[n])
             if 1 <= n <= ctx:
                 sum_pair(order[n - 1])
             if 3 <= n:
@@ -337,6 +372,15 @@
 
     for copy in sent:
         copy.wait_send()
+    for e, copy in skippable:
+        @pl.when(is_direct(e))
+        def _():
+            copy.wait_send()
+
+    for r, copy in relays:
+        @pl.when(me_ctx == r)
+        def _():
+            copy.wait_send()
 
 
 def fused_device(patches, carried, norm_gain, q_gain, k_gain, q_weight, k_weight, v_weight, o_weight):
@@ -362,6 +406,7 @@
             pltpu.VMEM((width, columns), bf16),
             pltpu.VMEM((width, columns), bf16),
             pltpu.VMEM((width, columns), bf16),
+            pltpu.VMEM((ctx, share, head_dim), bf16),
             pltpu.VMEM((columns, share), bf16),
             pltpu.VMEM((steps, ctx, 3, segment, head_dim), bf16),
             pltpu.VMEM((steps, 3, ctx, segment, head_dim), bf16),
@@ -382,7 +427,7 @@
             collective_id=0, has_side_effects=True, vmem_limit_bytes=56 * 2**20
         ),
         cost_estimate=pl.CostEstimate(flops=flops, bytes_accessed=12 * 2**20, transcendentals=0),
-    )(patches, carried, norm_gain, q_gain, k_gain, q_weight, k_weight, v_weight, o_weight)
+    )(patches, carried, norm_gain, q_gain, k_gain, q_weight, k_weight, v_weight, jnp.swapaxes(o_weight, 1, 2))
 
 
 def solution(mesh):
@@ -403,7 +448,7 @@
         ctx, mp, sections = mesh.shape["ctx"], mesh.shape["mp"], mesh.shape["section"]
         heads = arrays[5].shape[2] // arrays[3].shape[1]
         rows = arrays[1].shape[0] // (ctx * mp)
-        fits = mp == 4 and sections == 2 and ctx * mp == heads and ctx % 2 == 0 and rows == 16 * CHUNKS
+        fits = mp == 4 and sections == 2 and ctx * mp == heads and ctx == 4 and rows == 16 * CHUNKS
         body = fused_device if fits else per_device
         return jax.shard_map(body, mesh=mesh, in_specs=in_specs, out_specs=out_specs, check_vma=False)(*arrays)
 

time: 130 us -> 124 us (0.954)
  Pallas kernels: 126 us -> 121 us
  local copies, waits for them, and re-layouts: 4.15 us -> 1.94 us
    pallas_call x1, Pallas kernels: 126 us -> 121 us  [fused_device(): pl.pallas_call(functools.partial(layer_kernel, steps, ctx), out_shape=jax...]
    unnamed x2 -> x1, local copies, waits for them, and re-layouts: 4.15 us -> 1.94 us
where the time goes in v2:
time: 124 us; the launch traced here: 123 us
  Pallas kernels  121 us (98%)
  local copies, waits for them, and re-layouts  1.94 us (2%)
    pallas_call x1, Pallas kernels, fused_device(): pl.pallas_call(functools.partial(layer_kernel, steps, ctx), out_shape=jax...  121 us

profile of v2, /device:TPU:0, one launch (start us, length us, event | category | flops | bytes accessed | tf_op | source)
XLA Modules:
  0.0 122.6 jit_solution(9504595591522001382)
XLA Ops:
  0.0 120.6 %shard_map.91 = bf16[1,2,48,3200]{3,2,1,0:T(8,128)(2,1)} custom-call(bf16[2,48,3200]{2,1,0:T(8,128)(2,1)} %patches.1, bf16[48,3200]{1,0:T(8,128)(2,1)} %carried.1, f32[1,3200]{1,0:T(1,128)} %norm_gain.1, f32[1,128]{1,0:T(1,128)} %q_gain.1, f32[1,128]{1,0:T(1,128)} %k_gain.1, bf16[1,3200,512]{2,1,0:T(8,128)(2,1)} %q_weight.1, bf16[1,3200,512]{2,1,0:T(8,128)(2,1)} %k_weight.1, ...), custom_call_target="tpu_custom_call" | custom-call | flops 5637144576 | bytes 12582912 | tf_op jit(solution)/shard_map/pallas_call | solution.py:398
  120.7 1.9 %copy.11 = bf16[1,2,48,3200]{3,2,1,0:T(8,128)(2,1)} copy(bf16[1,2,48,3200]{3,2,1,0:T(8,128)(2,1)} %shard_map.91) | data formatting | bytes 1228800

commit v3 on v2

--- a/solution.py
+++ b/solution.py
@@ -132,9 +132,17 @@
     def _():
         pltpu.make_async_copy(carried, xg.at[0, 0], load_sems.at[0]).start()
 
+    head_order = [h for n in range(head_count // 2) for h in (n, head_count - 1 - n)]
     weight_loads = []
     for n, (source, target) in enumerate(((q_weight, wq), (k_weight, wk), (v_weight, wv))):
-        weight_loads.append(pltpu.make_async_copy(source.at[0], target, load_sems.at[steps + n]))
+        for place, h in enumerate(head_order):
+            weight_loads.append(
+                pltpu.make_async_copy(
+                    source.at[0, :, pl.ds(h * head_dim, head_dim)],
+                    target.at[:, pl.ds(place * head_dim, head_dim)],
+                    load_sems.at[2 * steps + 3 + ctx + n * head_count + place],
+                )
+            )
     out_loads = []
     for e in range(ctx):
         first = pl.multiple_of(ctx_at(-e) * head_dim, head_dim)
@@ -215,8 +223,9 @@
             raw = [
                 jnp.dot(normed[...], w[:, lanes], preferred_element_type=jnp.float32) for w in (wq, wk, wv)
             ]
-            for h in (first, first + 1):
-                own = slice((h - first) * head_dim, (h - first + 1) * head_dim)
+            for side in range(2):
+                h = head_order[first + side]
+                own = slice(side * head_dim, (side + 1) * head_dim)
                 parts = (
                     rms_scaled(raw[0][:, own], q_gain[...]).astype(jnp.bfloat16),
                     rms_scaled(raw[1][:, own], k_gain[...]).astype(jnp.bfloat16),
@@ -421,7 +430,7 @@
             pltpu.VMEM((steps, rows, width), bf16),
             pltpu.SemaphoreType.DMA((number,)),
             pltpu.SemaphoreType.DMA((number,)),
-            pltpu.SemaphoreType.DMA((2 * steps + 3 + ctx,)),
+            pltpu.SemaphoreType.DMA((2 * steps + 3 + ctx + 3 * (columns // head_dim),)),
         ],
         compiler_params=pltpu.CompilerParams(
             collective_id=0, has_side_effects=True, vmem_limit_bytes=56 * 2**20

time: 124 us -> 122 us (0.984)
  Pallas kernels: 121 us -> 119 us
where the time goes in v3:
time: 122 us; the launch traced here: 121 us
  Pallas kernels  119 us (98%)
  local copies, waits for them, and re-layouts  1.94 us (2%)
    pallas_call x1, Pallas kernels, fused_device(): pl.pallas_call(functools.partial(layer_kernel, steps, ctx), out_shape=jax...  119 us

profile of v3, /device:TPU:0, one launch (start us, length us, event | category | flops | bytes accessed | tf_op | source)
XLA Modules:
  0.0 121.4 jit_solution(3039916563610270608)
XLA Ops:
  0.0 119.4 %shard_map.91 = bf16[1,2,48,3200]{3,2,1,0:T(8,128)(2,1)} custom-call(bf16[2,48,3200]{2,1,0:T(8,128)(2,1)} %patches.1, bf16[48,3200]{1,0:T(8,128)(2,1)} %carried.1, f32[1,3200]{1,0:T(1,128)} %norm_gain.1, f32[1,128]{1,0:T(1,128)} %q_gain.1, f32[1,128]{1,0:T(1,128)} %k_gain.1, bf16[1,3200,512]{2,1,0:T(8,128)(2,1)} %q_weight.1, bf16[1,3200,512]{2,1,0:T(8,128)(2,1)} %k_weight.1, ...), custom_call_target="tpu_custom_call" | custom-call | flops 5637144576 | bytes 12582912 | tf_op jit(solution)/shard_map/pallas_call | solution.py:407
  119.4 1.9 %copy.11 = bf16[1,2,48,3200]{3,2,1,0:T(8,128)(2,1)} copy(bf16[1,2,48,3200]{3,2,1,0:T(8,128)(2,1)} %shard_map.91) | data formatting | bytes 1228800
